TPU v7x, 32 devices: a whole 2x2x4 slice. The times are simulated.
32 devices in a mesh: view: 2 (over y), tile: 16 (over z, x, core).
Axes of the slice: x: 2, y: 2, z: 4, core: 2. Of those that a mesh axis runs over, the one named last changes fastest.
Arguments:
- estimate: float32 [8, 512, 512], P(None, 'tile'), may hold values from 0.5 to 2
- observed: float32 [2, 8, 512, 512], P('view', None, 'tile'), may hold values from 0.2 to 4
- psf_taps: float32 [2, 3, 31], P('view'), may hold values from 0.05 to 1
Outputs:
- restored: float32 [8, 512, 512], P(None, 'tile')
All inputs are finite; a program needn't handle non-finite values.
Results may differ from a plain program's by a relative error of at most 0.0001.
Values sent between devices are 32-bit elements; how exact they have to be, the bound alone decides.
No kernel may reach another device: no remote copies, remote signals or barrier semaphores. Data moves between devices by JAX's collectives and lax.ppermute only.
A program may use at most 64 MiB of HBM per device.

v0:
```python
import jax
import jax.numpy as jnp
from jax import lax
from jax.sharding import PartitionSpec as P

ITERS = 2


def extended_2(cells, sides, width):
    for axis, dim in sides:
        count = lax.axis_size(axis)
        ends = count - 1
        head = lax.slice_in_dim(cells, 0, width, axis=dim)
        tail = lax.slice_in_dim(cells, cells.shape[dim] - width, cells.shape[dim], axis=dim)
        cells = jnp.concatenate(
            [
                lax.ppermute(tail, axis, [(i, (i + 1) % count) for i in range(ends)]),
                cells,
                lax.ppermute(head, axis, [((i + 1) % count, i) for i in range(ends)]),
            ],
            axis=dim,
        )
    return cells


def band_matrix(taps, count_in, count_out, offset):
    rows_in = jnp.arange(count_in)[:, None]
    cols_out = jnp.arange(count_out)[None, :]
    lag = rows_in - cols_out + offset
    length = taps.shape[0]
    inside = (lag >= 0) & (lag < length)
    return jnp.where(inside, jnp.take(taps, jnp.clip(lag, 0, length - 1)), 0.0)


def many_bands(taps, count_in, count_out, offset):
    return jax.vmap(lambda one: band_matrix(one, count_in, count_out, offset))(taps)


def blur(field, z_mats, y_mats, x_taps, cols_out):
    highest = lax.Precision.HIGHEST
    if field.ndim == 3:
        out = jnp.einsum("kyx,vkz->vzyx", field, z_mats, precision=highest)
    else:
        out = jnp.einsum("vkyx,vkz->vzyx", field, z_mats, precision=highest)
    out = jnp.einsum("vzjx,vjy->vzyx", out, y_mats, precision=highest)
    reach = (x_taps.shape[1] - 1) // 2
    pieces = []
    for start in range(0, cols_out, 128):
        block = min(128, cols_out - start)
        x_mats = many_bands(x_taps, block + 2 * reach, block, 0)
        piece = lax.slice_in_dim(out, start, start + block + 2 * reach, axis=3)
        pieces.append(jnp.einsum("vzyj,vjx->vzyx", piece, x_mats, precision=highest))
    return jnp.concatenate(pieces, axis=3)


def body(estimate, observed, psf_taps):
    depth, rows, width = estimate.shape
    half = (psf_taps.shape[2] - 1) // 2
    views = lax.axis_size("view")
    recorded = lax.all_to_all(observed, "view", split_axis=3, concat_axis=0, tiled=True)
    taps = lax.all_gather(psf_taps, "view", axis=0, tiled=True)
    cols = width // views
    col_start = lax.axis_index("view") * cols
    current = lax.dynamic_slice_in_dim(estimate, col_start, cols, 2)
    normed = taps / jnp.sum(taps, axis=2, keepdims=True)
    flipped = normed[:, :, ::-1]
    fwd_z = many_bands(normed[:, 0], depth, depth, half)
    back_z = many_bands(flipped[:, 0], depth, depth, half)
    back_y = many_bands(flipped[:, 1], rows + 2 * half, rows, 0)
    fwd_y = many_bands(normed[:, 1], rows + 2 * half, rows, 0)
    for step in range(ITERS):
        extended = extended_2(current, (("view", 2), ("tile", 1)), half)
        blurred = blur(extended, fwd_z, fwd_y, normed[:, 2], cols)
        ratio = recorded / blurred
        ratio_ext = extended_2(ratio, (("view", 3), ("tile", 2)), half)
        log_corr = jnp.log(blur(ratio_ext, back_z, back_y, flipped[:, 2], cols))
        log_total = jnp.sum(log_corr, axis=0)
        current = current * jnp.exp(log_total / views)
    current = lax.all_gather(current, "view", axis=2, tiled=True)
    return current


def solution(mesh):
    placed = (P(None, "tile", None), P("view", None, "tile", None), P("view", None, None))
    return jax.shard_map(
        body, mesh=mesh, in_specs=placed, out_specs=P(None, "tile", None), check_vma=False
    )
```

profile of v0, /device:TPU:19, one launch (start us, length us, event | category | flops | bytes accessed | tf_op | source)
XLA Modules:
  0.0 232.7 jit_solution(4656722165472639557)
XLA Ops:
  0.0 1.0 copy-done
  1.2 0.7 fusion.196
  2.0 3.8 %collective-permute-start = (f32[8,32,15]{2,0,1:T(8,128)}, f32[8,32,15]{2,0,1:T(8,128)}, u32[]{:S(2)}, u32[]{:S(2)}) collective-permute-start(f32[8,32,15]{2,0,1:T(8,128)} %get-tuple-element.22), channel_id=1, source_target_pairs={{0,16},{1,17},{2,18},{3,19},{4,20},{5,21},{6,22},{7,23},{8,24},{9,... | collective-permute-start | bytes 46088 | tf_op jit(solution)/shard_map/ppermute | solution.py:17
  5.8 1.3 collective-permute-start.1
  7.1 0.8 copy.103
  7.9 1.6 reshape.110
  9.5 4.0 %all-to-all-start = ((f32[2,1,65536]{2,1,0:T(1,128)}), f32[2,1,65536]{2,1,0:T(1,128)S(1)}, u32[]{:S(2)}, u32[]{:S(2)}) async-start(f32[2,1,65536]{2,1,0:T(1,128)} %reshape.110), calls=%async_computation | async-start | bytes 1048576 | tf_op jit(solution)/shard_map/all_to_all | solution.py:60
  13.6 7.8 %all_gather.6 = f32[2,3,31]{2,1,0:T(4,128)S(1)} all-gather(f32[1,3,31]{2,1,0:T(4,128)S(1)} %copy.97), channel_id=1, replica_groups=mesh['view'=2,'tile'=16] {'view'}, dimensions={0}, use_global_device_ids=true | all-gather | bytes 1116 | tf_op jit(solution)/shard_map/all_gather | solution.py:61
  21.9 1.1 pad_maximum_fusion.9
  23.1 5.0 %collective-permute-start.2 = (f32[8,15,286]{2,0,1:T(8,128)S(1)}, f32[8,15,286]{2,0,1:T(8,128)S(1)}, u32[]{:S(2)}, u32[]{:S(2)}) collective-permute-start(f32[8,15,286]{2,0,1:T(8,128)S(1)} %get-tuple-element.18), channel_id=1, source_target_pairs={{0,1},{1,2},{2,3},{3,4},{4,5},{5,6},{6,7},{7,8},{8,9},{9,10},{10,1... | collective-permute-start | bytes 411848 | tf_op jit(solution)/shard_map/ppermute | solution.py:17
  28.0 1.9 collective-permute-start.3
  31.0 5.6 %gather_fusion.2 = f32[1984,2]{1,0:T(8,128)S(1)} fusion(f32[2,31]{0,1:T(8,128)S(1)} %copy.107, s32[2048]{0:T(1024)S(1)} %pad_clamp_fusion.1), kind=kCustom, calls=%fused_computation.3.clone | custom fusion | bytes 39680 | tf_op jit(solution)/shard_map/vmap(jit(_take))/gather | solution.py:32
  36.5 0.7 copy.108
  37.2 37.8 %gather_fusion.4 = f32[20224,2]{1,0:T(8,128)} fusion(f32[2,31]{0,1:T(8,128)S(1)} %copy.113, s32[20480]{0:T(1024)S(1)} %pad_clamp_fusion), kind=kCustom, calls=%fused_computation.2.clone | custom fusion | bytes 404480 | tf_op jit(solution)/shard_map/vmap(jit(_take))/gather | solution.py:32
  75.0 6.0 %copy.114 = f32[158,128,2]{1,0,2:T(8,128)S(1)} copy(f32[158,128,2]{2,1,0:T(8,128)} %bitcast.150) | data formatting | bytes 323584 | tf_op jit(solution)/shard_map/vmap(jit(_take))/gather | solution.py:32
  81.1 2.5 %fusion.24 = f32[2,8,62,286]{3,1,2,0:T(8,128)S(1)} fusion(f32[8,15,286]{2,0,1:T(8,128)} %collective-permute-done.3, f32[8,32,15]{2,0,1:T(8,128)} %collective-permute-done.1, f32[8,32,256]{2,0,1:T(8,128)S(1)} %copy.148, f32[8,32,15]{2,0,1:T(8,128)} %collective-permute-done, f32[8,15,286]{2,0,1:T(8,128)S(1)} %collective-permute-done.2, ...), kind=kOutput, calls=%fused_computation.27 | convolution fusion | flops 27804032 | bytes 1702912 | tf_op jit(solution)/shard_map/kyx,vkz->vzyx/dot_general | solution.py:42
  83.6 1.1 fusion.12
  84.7 1.3 fusion.54
  86.0 1.3 fusion.56
  87.8 2.3 reduce
  90.2 0.9 reshape.111
  91.0 0.6 copy.105
  91.7 1.1 maximum_divide_fusion
  92.9 1.4 collective-permute-start.4
  94.4 1.3 collective-permute-start.5
  95.7 3.8 %collective-permute-done.4 = f32[2,8,32,15]{3,2,1,0:T(8,128)S(1)} collective-permute-done((f32[2,8,32,15]{3,2,1,0:T(8,128)S(1)}, f32[2,8,32,15]{3,2,1,0:T(8,128)S(1)}, u32[]{:S(2)}, u32[]{:S(2)}) %collective-permute-start.4) | collective-permute-done | bytes 30752 | tf_op jit(solution)/shard_map/ppermute | solution.py:17
  99.4 3.8 %collective-permute-done.5 = f32[2,8,32,15]{3,2,1,0:T(8,128)S(1)} collective-permute-done((f32[2,8,32,15]{3,2,1,0:T(8,128)S(1)}, f32[2,8,32,15]{3,2,1,0:T(8,128)S(1)}, u32[]{:S(2)}, u32[]{:S(2)}) %collective-permute-start.5) | collective-permute-done | bytes 30752 | tf_op jit(solution)/shard_map/ppermute | solution.py:19
  103.6 1.0 fusion.192
  104.6 4.7 %collective-permute-start.6 = (f32[2,8,15,286]{3,2,1,0:T(8,128)}, f32[2,8,15,286]{3,2,1,0:T(8,128)}, u32[]{:S(2)}, u32[]{:S(2)}) collective-permute-start(f32[2,8,15,286]{3,2,1,0:T(8,128)} %get-tuple-element.10), channel_id=1, source_target_pairs={{0,1},{1,2},{2,3},{3,4},{4,5},{5,6},{6,7},{7,8},{8,9},{9,10},{10,1... | collective-permute-start | bytes 823688 | tf_op jit(solution)/shard_map/ppermute | solution.py:17
  109.3 2.1 collective-permute-start.7
  112.7 5.6 %gather_fusion = f32[1984,2]{1,0:T(8,128)S(1)} fusion(f32[2,31]{0,1:T(8,128)S(1)} %copy.99, s32[2048]{0:T(1024)S(1)} %pad_clamp_fusion.1), kind=kCustom, calls=%fused_computation.clone | custom fusion | bytes 39680 | tf_op jit(solution)/shard_map/vmap(jit(_take))/gather | solution.py:32
  118.3 0.7 copy.100
  118.9 37.8 %gather_fusion.5 = f32[20224,2]{1,0:T(8,128)} fusion(f32[2,31]{0,1:T(8,128)S(1)} %copy.118, s32[20480]{0:T(1024)S(1)} %pad_clamp_fusion), kind=kCustom, calls=%fused_computation.5.clone | custom fusion | bytes 404480 | tf_op jit(solution)/shard_map/vmap(jit(_take))/gather | solution.py:32
  156.7 6.0 %copy.119 = f32[158,128,2]{1,0,2:T(8,128)S(1)} copy(f32[158,128,2]{2,1,0:T(8,128)} %bitcast.149) | data formatting | bytes 323584 | tf_op jit(solution)/shard_map/vmap(jit(_take))/gather | solution.py:32
  162.7 1.5 pad_maximum_fusion
  164.3 2.1 fusion.10
  166.4 1.1 fusion.15
  167.6 0.6 fusion.50
  168.2 0.6 fusion.52
  169.3 1.3 collective-permute-start.8
  170.6 1.3 collective-permute-start.9
  171.9 1.0 collective-permute-done.8
  172.9 3.8 %collective-permute-done.9 = f32[8,32,15]{2,0,1:T(8,128)S(1)} collective-permute-done((f32[8,32,15]{2,0,1:T(8,128)S(1)}, f32[8,32,15]{2,0,1:T(8,128)S(1)}, u32[]{:S(2)}, u32[]{:S(2)}) %collective-permute-start.9) | collective-permute-done | bytes 15392 | tf_op jit(solution)/shard_map/ppermute | solution.py:19
  177.0 5.4 %collective-permute-start.10 = (f32[8,15,286]{2,0,1:T(8,128)S(1)}, f32[8,15,286]{2,0,1:T(8,128)S(1)}, u32[]{:S(2)}, u32[]{:S(2)}) collective-permute-start(f32[8,15,286]{2,0,1:T(8,128)S(1)} %get-tuple-element.14), channel_id=1, source_target_pairs={{0,1},{1,2},{2,3},{3,4},{4,5},{5,6},{6,7},{7,8},{8,9},{9,10},{10,1... | collective-permute-start | bytes 411848 | tf_op jit(solution)/shard_map/ppermute | solution.py:17
  182.4 1.9 collective-permute-start.11
  184.9 5.3 %collective-permute-done.11 = f32[8,15,286]{2,0,1:T(8,128)S(1)} collective-permute-done((f32[8,15,286]{2,0,1:T(8,128)S(1)}, f32[8,15,286]{2,0,1:T(8,128)S(1)}, u32[]{:S(2)}, u32[]{:S(2)}) %collective-permute-start.11) | collective-permute-done | bytes 137312 | tf_op jit(solution)/shard_map/ppermute | solution.py:19
  190.2 1.4 fusion.33
  191.6 1.1 fusion.18
  192.7 0.6 fusion.46
  193.3 0.6 fusion.48
  194.2 1.3 collective-permute-start.12
  195.5 1.3 collective-permute-start.13
  196.8 2.2 collective-permute-done.12
  199.0 4.1 %collective-permute-done.13 = f32[2,8,32,15]{3,2,1,0:T(8,128)S(1)} collective-permute-done((f32[2,8,32,15]{3,2,1,0:T(8,128)S(1)}, f32[2,8,32,15]{3,2,1,0:T(8,128)S(1)}, u32[]{:S(2)}, u32[]{:S(2)}) %collective-permute-start.13) | collective-permute-done | bytes 30752 | tf_op jit(solution)/shard_map/ppermute | solution.py:19
  203.5 4.3 %collective-permute-start.14 = (f32[2,8,15,286]{3,2,1,0:T(8,128)S(1)}, f32[2,8,15,286]{3,2,1,0:T(8,128)S(1)}, u32[]{:S(2)}, u32[]{:S(2)}) collective-permute-start(f32[2,8,15,286]{3,2,1,0:T(8,128)S(1)} %get-tuple-element.6), channel_id=1, source_target_pairs={{0,1},{1,2},{2,3},{3,4},{4,5},{5,6},{6,7},{7,8},{8,9},{9,10},{10,1... | collective-permute-start | bytes 823688 | tf_op jit(solution)/shard_map/ppermute | solution.py:17
  207.8 2.1 collective-permute-start.15
  210.0 2.6 %collective-permute-done.14 = f32[2,8,15,286]{3,2,1,0:T(8,128)S(1)} collective-permute-done((f32[2,8,15,286]{3,2,1,0:T(8,128)S(1)}, f32[2,8,15,286]{3,2,1,0:T(8,128)S(1)}, u32[]{:S(2)}, u32[]{:S(2)}) %collective-permute-start.14) | collective-permute-done | bytes 274592 | tf_op jit(solution)/shard_map/ppermute | solution.py:17
  212.6 5.3 %collective-permute-done.15 = f32[2,8,15,286]{3,2,1,0:T(8,128)S(1)} collective-permute-done((f32[2,8,15,286]{3,2,1,0:T(8,128)S(1)}, f32[2,8,15,286]{3,2,1,0:T(8,128)S(1)}, u32[]{:S(2)}, u32[]{:S(2)}) %collective-permute-start.15) | collective-permute-done | bytes 274592 | tf_op jit(solution)/shard_map/ppermute | solution.py:19
  218.3 2.1 fusion.8
  220.4 1.1 fusion.21
  221.5 0.6 fusion.42
  222.2 0.6 fusion.44
  223.1 8.6 %all_gather.7 = f32[8,32,512]{2,0,1:T(8,128)S(1)} all-gather(f32[8,32,256]{2,0,1:T(8,128)S(1)} %fusion.61), channel_id=1, replica_groups=mesh['view'=2,'tile'=16] {'view'}, dimensions={2}, use_global_device_ids=true | all-gather | bytes 786432 | tf_op jit(solution)/shard_map/all_gather | solution.py:79
  231.6 1.1 copy.127
  (62 shorter events, 6.7 us)
Async XLA Ops:
  0.0 1.0 copy-start
  0.0 7.1 %copy-start.3 = (f32[1,8,32,512]{3,2,1,0:T(8,128)S(1)}, f32[1,8,32,512]{3,2,1,0:T(8,128)}, u32[]{:S(2)}) copy-start(f32[1,8,32,512]{3,2,1,0:T(8,128)} %param.10) | copy-start | bytes 1572868
  1.1 4.7 %copy-start.1 = (f32[8,32,256]{2,1,0:T(8,128)}, f32[8,32,256]{2,1,0:T(8,128)S(1)}, u32[]{:S(2)}) copy-start(f32[8,32,256]{2,1,0:T(8,128)S(1)} %constant_dynamic-slice_fusion) | copy-start | bytes 786436
  2.0 19.9 %collective-permute-start = (f32[8,32,15]{2,0,1:T(8,128)}, f32[8,32,15]{2,0,1:T(8,128)}, u32[]{:S(2)}, u32[]{:S(2)}) collective-permute-start(f32[8,32,15]{2,0,1:T(8,128)} %get-tuple-element.22), channel_id=1, source_target_pairs={{0,16},{1,17},{2,18},{3,19},{4,20},{5,21},{6,22},{7,23},{8,24},{9,... | collective-permute-start | bytes 46088 | tf_op jit(solution)/shard_map/ppermute | solution.py:17
  5.8 16.1 %collective-permute-start.1 = (f32[8,32,15]{2,0,1:T(8,128)}, f32[8,32,15]{2,0,1:T(8,128)}, u32[]{:S(2)}, u32[]{:S(2)}) collective-permute-start(f32[8,32,15]{2,0,1:T(8,128)} %get-tuple-element.23), channel_id=1, source_target_pairs={{16,0},{17,1},{18,2},{19,3},{20,4},{21,5},{22,6},{23,7},{24,8},{25... | collective-permute-start | bytes 46088 | tf_op jit(solution)/shard_map/ppermute | solution.py:19
  7.9 5.7 %copy-start.4 = (f32[1,3,31]{2,0,1:T(1,128)S(1)}, f32[1,3,31]{2,0,1:T(1,128)}, u32[]{:S(2)}) copy-start(f32[1,3,31]{2,0,1:T(1,128)} %param.11) | copy-start | bytes 1120
  9.5 77.8 %all-to-all-start = ((f32[2,1,65536]{2,1,0:T(1,128)}), f32[2,1,65536]{2,1,0:T(1,128)S(1)}, u32[]{:S(2)}, u32[]{:S(2)}) async-start(f32[2,1,65536]{2,1,0:T(1,128)} %reshape.110), calls=%async_computation | async-start | bytes 1048576 | tf_op jit(solution)/shard_map/all_to_all | solution.py:60
  23.1 58.0 %collective-permute-start.2 = (f32[8,15,286]{2,0,1:T(8,128)S(1)}, f32[8,15,286]{2,0,1:T(8,128)S(1)}, u32[]{:S(2)}, u32[]{:S(2)}) collective-permute-start(f32[8,15,286]{2,0,1:T(8,128)S(1)} %get-tuple-element.18), channel_id=1, source_target_pairs={{0,1},{1,2},{2,3},{3,4},{4,5},{5,6},{6,7},{7,8},{8,9},{9,10},{10,1... | collective-permute-start | bytes 411848 | tf_op jit(solution)/shard_map/ppermute | solution.py:17
  28.0 53.1 %collective-permute-start.3 = (f32[8,15,286]{2,0,1:T(8,128)S(1)}, f32[8,15,286]{2,0,1:T(8,128)}, u32[]{:S(2)}, u32[]{:S(2)}) collective-permute-start(f32[8,15,286]{2,0,1:T(8,128)S(1)} %get-tuple-element.19), channel_id=1, source_target_pairs={{1,0},{2,1},{3,2},{4,3},{5,4},{6,5},{7,6},{8,7},{9,8},{10,9},{11,1... | collective-permute-start | bytes 411848 | tf_op jit(solution)/shard_map/ppermute | solution.py:19
  92.9 6.5 %collective-permute-start.4 = (f32[2,8,32,15]{3,2,1,0:T(8,128)S(1)}, f32[2,8,32,15]{3,2,1,0:T(8,128)S(1)}, u32[]{:S(2)}, u32[]{:S(2)}) collective-permute-start(f32[2,8,32,15]{3,2,1,0:T(8,128)S(1)} %get-tuple-element.16), channel_id=1, source_target_pairs={{0,16},{1,17},{2,18},{3,19},{4,20},{5,21},{6,22},{7,23},{8,24},{9,... | collective-permute-start | bytes 92168 | tf_op jit(solution)/shard_map/ppermute | solution.py:17
  94.4 8.9 %collective-permute-start.5 = (f32[2,8,32,15]{3,2,1,0:T(8,128)S(1)}, f32[2,8,32,15]{3,2,1,0:T(8,128)S(1)}, u32[]{:S(2)}, u32[]{:S(2)}) collective-permute-start(f32[2,8,32,15]{3,2,1,0:T(8,128)S(1)} %get-tuple-element.17), channel_id=1, source_target_pairs={{16,0},{17,1},{18,2},{19,3},{20,4},{21,5},{22,6},{23,7},{24,8},{25... | collective-permute-start | bytes 92168 | tf_op jit(solution)/shard_map/ppermute | solution.py:19
  104.6 58.2 %collective-permute-start.6 = (f32[2,8,15,286]{3,2,1,0:T(8,128)}, f32[2,8,15,286]{3,2,1,0:T(8,128)}, u32[]{:S(2)}, u32[]{:S(2)}) collective-permute-start(f32[2,8,15,286]{3,2,1,0:T(8,128)} %get-tuple-element.10), channel_id=1, source_target_pairs={{0,1},{1,2},{2,3},{3,4},{4,5},{5,6},{6,7},{7,8},{8,9},{9,10},{10,1... | collective-permute-start | bytes 823688 | tf_op jit(solution)/shard_map/ppermute | solution.py:17
  109.3 53.4 %collective-permute-start.7 = (f32[2,8,15,286]{3,2,1,0:T(8,128)}, f32[2,8,15,286]{3,2,1,0:T(8,128)}, u32[]{:S(2)}, u32[]{:S(2)}) collective-permute-start(f32[2,8,15,286]{3,2,1,0:T(8,128)} %get-tuple-element.11), channel_id=1, source_target_pairs={{1,0},{2,1},{3,2},{4,3},{5,4},{6,5},{7,6},{8,7},{9,8},{10,9},{11,1... | collective-permute-start | bytes 823688 | tf_op jit(solution)/shard_map/ppermute | solution.py:19
  167.5 1.3 copy-start.2
  169.3 3.6 %collective-permute-start.8 = (f32[8,32,15]{2,0,1:T(8,128)S(1)}, f32[8,32,15]{2,0,1:T(8,128)S(1)}, u32[]{:S(2)}, u32[]{:S(2)}) collective-permute-start(f32[8,32,15]{2,0,1:T(8,128)S(1)} %get-tuple-element.20), channel_id=1, source_target_pairs={{0,16},{1,17},{2,18},{3,19},{4,20},{5,21},{6,22},{7,23},{8,24},{9,... | collective-permute-start | bytes 46088 | tf_op jit(solution)/shard_map/ppermute | solution.py:17
  170.6 6.2 %collective-permute-start.9 = (f32[8,32,15]{2,0,1:T(8,128)S(1)}, f32[8,32,15]{2,0,1:T(8,128)S(1)}, u32[]{:S(2)}, u32[]{:S(2)}) collective-permute-start(f32[8,32,15]{2,0,1:T(8,128)S(1)} %get-tuple-element.21), channel_id=1, source_target_pairs={{16,0},{17,1},{18,2},{19,3},{20,4},{21,5},{22,6},{23,7},{24,8},{25... | collective-permute-start | bytes 46088 | tf_op jit(solution)/shard_map/ppermute | solution.py:19
  177.0 7.9 %collective-permute-start.10 = (f32[8,15,286]{2,0,1:T(8,128)S(1)}, f32[8,15,286]{2,0,1:T(8,128)S(1)}, u32[]{:S(2)}, u32[]{:S(2)}) collective-permute-start(f32[8,15,286]{2,0,1:T(8,128)S(1)} %get-tuple-element.14), channel_id=1, source_target_pairs={{0,1},{1,2},{2,3},{3,4},{4,5},{5,6},{6,7},{7,8},{8,9},{9,10},{10,1... | collective-permute-start | bytes 411848 | tf_op jit(solution)/shard_map/ppermute | solution.py:17
  182.4 7.8 %collective-permute-start.11 = (f32[8,15,286]{2,0,1:T(8,128)S(1)}, f32[8,15,286]{2,0,1:T(8,128)S(1)}, u32[]{:S(2)}, u32[]{:S(2)}) collective-permute-start(f32[8,15,286]{2,0,1:T(8,128)S(1)} %get-tuple-element.15), channel_id=1, source_target_pairs={{1,0},{2,1},{3,2},{4,3},{5,4},{6,5},{7,6},{8,7},{9,8},{10,9},{11,1... | collective-permute-start | bytes 411848 | tf_op jit(solution)/shard_map/ppermute | solution.py:19
  194.2 4.8 %collective-permute-start.12 = (f32[2,8,32,15]{3,2,1,0:T(8,128)S(1)}, f32[2,8,32,15]{3,2,1,0:T(8,128)S(1)}, u32[]{:S(2)}, u32[]{:S(2)}) collective-permute-start(f32[2,8,32,15]{3,2,1,0:T(8,128)S(1)} %get-tuple-element.12), channel_id=1, source_target_pairs={{0,16},{1,17},{2,18},{3,19},{4,20},{5,21},{6,22},{7,23},{8,24},{9,... | collective-permute-start | bytes 92168 | tf_op jit(solution)/shard_map/ppermute | solution.py:17
  195.5 7.6 %collective-permute-start.13 = (f32[2,8,32,15]{3,2,1,0:T(8,128)S(1)}, f32[2,8,32,15]{3,2,1,0:T(8,128)S(1)}, u32[]{:S(2)}, u32[]{:S(2)}) collective-permute-start(f32[2,8,32,15]{3,2,1,0:T(8,128)S(1)} %get-tuple-element.13), channel_id=1, source_target_pairs={{16,0},{17,1},{18,2},{19,3},{20,4},{21,5},{22,6},{23,7},{24,8},{25... | collective-permute-start | bytes 92168 | tf_op jit(solution)/shard_map/ppermute | solution.py:19
  203.5 9.0 %collective-permute-start.14 = (f32[2,8,15,286]{3,2,1,0:T(8,128)S(1)}, f32[2,8,15,286]{3,2,1,0:T(8,128)S(1)}, u32[]{:S(2)}, u32[]{:S(2)}) collective-permute-start(f32[2,8,15,286]{3,2,1,0:T(8,128)S(1)} %get-tuple-element.6), channel_id=1, source_target_pairs={{0,1},{1,2},{2,3},{3,4},{4,5},{5,6},{6,7},{7,8},{8,9},{9,10},{10,1... | collective-permute-start | bytes 823688 | tf_op jit(solution)/shard_map/ppermute | solution.py:17
  207.8 10.0 %collective-permute-start.15 = (f32[2,8,15,286]{3,2,1,0:T(8,128)S(1)}, f32[2,8,15,286]{3,2,1,0:T(8,128)S(1)}, u32[]{:S(2)}, u32[]{:S(2)}) collective-permute-start(f32[2,8,15,286]{3,2,1,0:T(8,128)S(1)} %get-tuple-element.8), channel_id=1, source_target_pairs={{1,0},{2,1},{3,2},{4,3},{5,4},{6,5},{7,6},{8,7},{9,8},{10,9},{11,1... | collective-permute-start | bytes 823688 | tf_op jit(solution)/shard_map/ppermute | solution.py:19
where the time goes:
time: 233 us
  local copies, waits for them, and re-layouts  111 us (48%)
  starting transfers between devices  44.4 us (19%)
  waiting for transfers between devices  32.5 us (14%)
  matrix products  18.9 us (8%)
  blocking collectives  16.4 us (7%)
  other arithmetic  8.52 us (4%)
    gather x12, local copies, waits for them, and re-layouts, band_matrix(): return jnp.where(inside, jnp.take(taps, jnp.clip(lag, 0, length - 1)), 0.0)  101 us
    ppermute x8, starting transfers between devices, extended_2(): lax.ppermute(tail, axis, [(i, (i + 1) % count) for i in range(ends)])  27.2 us
    ppermute x8, waiting for transfers between devices, extended_2(): lax.ppermute(head, axis, [((i + 1) % count, i) for i in range(ends)])  22.4 us
    ppermute x8, starting transfers between devices, extended_2(): lax.ppermute(head, axis, [((i + 1) % count, i) for i in range(ends)])  13.2 us
    ppermute x8, waiting for transfers between devices, extended_2(): lax.ppermute(tail, axis, [(i, (i + 1) % count) for i in range(ends)])  10.1 us
    all_gather x1, blocking collectives, body(): current = lax.all_gather(current, 'view', axis=2, tiled=True)  8.58 us
    all_gather x1, blocking collectives, body(): taps = lax.all_gather(psf_taps, 'view', axis=0, tiled=True)  7.85 us
    dot_general x8, matrix products, blur(): jnp.einsum('vzyj,vjx->vzyx', piece, x_mats, precision=highest)  6.3 us
  transfers between devices with their start and end apart: 17, of which 10 were waited for; matrix products, arithmetic and copies ran while one was open for 48% of the time, Pallas kernels for 0%

commit v1 on v0

--- a/solution.py
+++ b/solution.py
@@ -57,7 +57,10 @@
     depth, rows, width = estimate.shape
     half = (psf_taps.shape[2] - 1) // 2
     views = lax.axis_size("view")
-    recorded = lax.all_to_all(observed, "view", split_axis=3, concat_axis=0, tiled=True)
+    recorded = jnp.concatenate(
+        lax.all_to_all(jnp.stack(jnp.split(observed, lax.axis_size("view"), axis=3)), "view", 0, 0),
+        axis=0,
+    )
     taps = lax.all_gather(psf_taps, "view", axis=0, tiled=True)
     cols = width // views
     col_start = lax.axis_index("view") * cols

time: 233 us -> 224 us (0.961)
  local copies, waits for them, and re-layouts: 111 us -> 108 us
  other arithmetic: 8.52 us -> 5.81 us
    unnamed x15 -> x28, local copies, waits for them, and re-layouts: 4.48 us -> 1.25 us
  transfers between devices with their start and end apart: 17 -> 17, of which waited for: 10 -> 10; matrix products, arithmetic and copies ran while one was open for 48% -> 49% of each run, Pallas kernels for 0% -> 0%
where the time goes in v1:
time: 224 us
  local copies, waits for them, and re-layouts  108 us (48%)
  starting transfers between devices  43.2 us (19%)
  waiting for transfers between devices  32.5 us (15%)
  matrix products  17.5 us (8%)
  blocking collectives  16.3 us (7%)
  other arithmetic  5.81 us (3%)
    gather x12, local copies, waits for them, and re-layouts, band_matrix(): return jnp.where(inside, jnp.take(taps, jnp.clip(lag, 0, length - 1)), 0.0)  103 us
    ppermute x8, starting transfers between devices, extended_2(): lax.ppermute(tail, axis, [(i, (i + 1) % count) for i in range(ends)])  26.5 us
    ppermute x8, waiting for transfers between devices, extended_2(): lax.ppermute(head, axis, [((i + 1) % count, i) for i in range(ends)])  22.4 us
    ppermute x8, starting transfers between devices, extended_2(): lax.ppermute(head, axis, [((i + 1) % count, i) for i in range(ends)])  13.3 us
    ppermute x8, waiting for transfers between devices, extended_2(): lax.ppermute(tail, axis, [(i, (i + 1) % count) for i in range(ends)])  10.1 us
    all_gather x1, blocking collectives, body(): current = lax.all_gather(current, 'view', axis=2, tiled=True)  8.59 us
    all_gather x1, blocking collectives, body(): taps = lax.all_gather(psf_taps, 'view', axis=0, tiled=True)  7.69 us
    dot_general x8, matrix products, blur(): jnp.einsum('vzyj,vjx->vzyx', piece, x_mats, precision=highest)  4.9 us
  transfers between devices with their start and end apart: 17, of which 10 were waited for; matrix products, arithmetic and copies ran while one was open for 49% of the time, Pallas kernels for 0%

profile of v1, /device:TPU:19, one launch (start us, length us, event | category | flops | bytes accessed | tf_op | source)
XLA Modules:
  0.0 223.7 jit_solution(18413798909415409846)
XLA Ops:
  0.0 1.0 copy-done
  1.3 3.2 %collective-permute-start = (f32[8,32,15]{2,0,1:T(8,128)S(1)}, f32[8,32,15]{2,0,1:T(8,128)S(1)}, u32[]{:S(2)}, u32[]{:S(2)}) collective-permute-start(f32[8,32,15]{2,0,1:T(8,128)S(1)} %get-tuple-element.24), channel_id=1, source_target_pairs={{0,16},{1,17},{2,18},{3,19},{4,20},{5,21},{6,22},{7,23},{8,24},{9,... | collective-permute-start | bytes 46088 | tf_op jit(solution)/shard_map/ppermute | solution.py:17
  4.5 1.3 collective-permute-start.1
  5.9 0.8 pad_maximum_fusion.4
  6.7 3.5 %all-to-all-start = ((f32[2,1,8,32,256]{4,3,2,1,0:T(8,128)}), f32[2,1,8,32,256]{4,3,2,1,0:T(8,128)S(1)}, u32[]{:S(2)}, u32[]{:S(2)}) async-start(f32[2,1,8,32,256]{4,3,2,1,0:T(8,128)} %pad_maximum_fusion.4), calls=%async_computation | async-start | bytes 1048576 | tf_op jit(solution)/shard_map/all_to_all | solution.py:61
  10.3 7.7 %all_gather.6 = f32[2,3,31]{2,1,0:T(4,128)S(1)} all-gather(f32[1,3,31]{2,1,0:T(4,128)S(1)} %copy.90), channel_id=1, replica_groups=mesh['view'=2,'tile'=16] {'view'}, dimensions={0}, use_global_device_ids=true | all-gather | bytes 1116 | tf_op jit(solution)/shard_map/all_gather | solution.py:64
  18.5 0.8 pad_maximum_fusion.10
  19.4 4.9 %collective-permute-start.2 = (f32[8,15,286]{2,0,1:T(8,128)}, f32[8,15,286]{2,0,1:T(8,128)}, u32[]{:S(2)}, u32[]{:S(2)}) collective-permute-start(f32[8,15,286]{2,0,1:T(8,128)} %get-tuple-element.20), channel_id=1, source_target_pairs={{0,1},{1,2},{2,3},{3,4},{4,5},{5,6},{6,7},{7,8},{8,9},{9,10},{10,1... | collective-permute-start | bytes 411848 | tf_op jit(solution)/shard_map/ppermute | solution.py:17
  24.3 1.9 collective-permute-start.3
  26.5 0.6 gather_fusion.3
  27.3 5.6 %gather_fusion.2 = f32[1984,2]{1,0:T(8,128)S(1)} fusion(f32[2,31]{0,1:T(8,128)S(1)} %copy.97, s32[2048]{0:T(1024)S(1)} %pad_clamp_fusion.1), kind=kCustom, calls=%fused_computation.3.clone | custom fusion | bytes 39680 | tf_op jit(solution)/shard_map/vmap(jit(_take))/gather | solution.py:32
  32.9 0.7 copy.98
  33.5 37.8 %gather_fusion.4 = f32[20224,2]{1,0:T(8,128)} fusion(f32[2,31]{0,1:T(8,128)S(1)} %copy.103, s32[20480]{0:T(1024)S(1)} %pad_clamp_fusion), kind=kCustom, calls=%fused_computation.2.clone | custom fusion | bytes 404480 | tf_op jit(solution)/shard_map/vmap(jit(_take))/gather | solution.py:32
  71.4 6.0 %copy.104 = f32[158,128,2]{1,0,2:T(8,128)S(1)} copy(f32[158,128,2]{2,1,0:T(8,128)} %bitcast.149) | data formatting | bytes 323584 | tf_op jit(solution)/shard_map/vmap(jit(_take))/gather | solution.py:32
  77.4 2.4 %fusion.24 = f32[2,8,62,286]{3,1,2,0:T(8,128)S(1)} fusion(f32[8,15,286]{2,0,1:T(8,128)} %collective-permute-done.3, f32[8,32,15]{2,0,1:T(8,128)S(1)} %collective-permute-done.1, f32[8,32,256]{2,0,1:T(8,128)S(1)} %copy.136, f32[8,32,15]{2,0,1:T(8,128)S(1)} %collective-permute-done, f32[8,15,286]{2,0,1:T(8,128)} %collective-permute-done.2, ...), kind=kOutput, calls=%fused_computation.27 | convolution fusion | flops 27804032 | bytes 1702912 | tf_op jit(solution)/shard_map/kyx,vkz->vzyx/dot_general | solution.py:42
  79.9 1.1 fusion.12
  81.0 0.6 fusion.54
  81.6 0.6 fusion.56
  82.5 1.4 collective-permute-start.4
  83.9 1.3 collective-permute-start.5
  85.2 3.8 %collective-permute-done.4 = f32[2,8,32,15]{3,2,1,0:T(8,128)S(1)} collective-permute-done((f32[2,8,32,15]{3,2,1,0:T(8,128)S(1)}, f32[2,8,32,15]{3,2,1,0:T(8,128)S(1)}, u32[]{:S(2)}, u32[]{:S(2)}) %collective-permute-start.4) | collective-permute-done | bytes 30752 | tf_op jit(solution)/shard_map/ppermute | solution.py:17
  89.0 3.8 %collective-permute-done.5 = f32[2,8,32,15]{3,2,1,0:T(8,128)S(1)} collective-permute-done((f32[2,8,32,15]{3,2,1,0:T(8,128)S(1)}, f32[2,8,32,15]{3,2,1,0:T(8,128)S(1)}, u32[]{:S(2)}, u32[]{:S(2)}) %collective-permute-start.5) | collective-permute-done | bytes 30752 | tf_op jit(solution)/shard_map/ppermute | solution.py:19
  92.8 0.3 pad_maximum_fusion.2
  93.2 1.0 fusion.192
  94.2 4.7 %collective-permute-start.6 = (f32[2,8,15,286]{3,2,1,0:T(8,128)}, f32[2,8,15,286]{3,2,1,0:T(8,128)}, u32[]{:S(2)}, u32[]{:S(2)}) collective-permute-start(f32[2,8,15,286]{3,2,1,0:T(8,128)} %get-tuple-element.10), channel_id=1, source_target_pairs={{0,1},{1,2},{2,3},{3,4},{4,5},{5,6},{6,7},{7,8},{8,9},{9,10},{10,1... | collective-permute-start | bytes 823688 | tf_op jit(solution)/shard_map/ppermute | solution.py:17
  98.9 2.1 collective-permute-start.7
  101.6 0.6 gather_fusion.1
  102.2 0.7 copy.126
  102.9 5.6 %gather_fusion = f32[1984,2]{1,0:T(8,128)S(1)} fusion(f32[2,31]{0,1:T(8,128)S(1)} %copy.92, s32[2048]{0:T(1024)S(1)} %pad_clamp_fusion.1), kind=kCustom, calls=%fused_computation.clone | custom fusion | bytes 39680 | tf_op jit(solution)/shard_map/vmap(jit(_take))/gather | solution.py:32
  108.4 1.3 copy.93
  109.7 37.8 %gather_fusion.5 = f32[20224,2]{1,0:T(8,128)} fusion(f32[2,31]{0,1:T(8,128)S(1)} %copy.108, s32[20480]{0:T(1024)S(1)} %pad_clamp_fusion), kind=kCustom, calls=%fused_computation.5.clone | custom fusion | bytes 404480 | tf_op jit(solution)/shard_map/vmap(jit(_take))/gather | solution.py:32
  147.5 6.0 %copy.109 = f32[158,128,2]{1,0,2:T(8,128)S(1)} copy(f32[158,128,2]{2,1,0:T(8,128)} %bitcast.148) | data formatting | bytes 323584 | tf_op jit(solution)/shard_map/vmap(jit(_take))/gather | solution.py:32
  153.6 1.6 pad_maximum_fusion
  155.2 2.1 fusion.10
  157.3 1.1 fusion.15
  158.5 0.6 fusion.50
  159.1 0.6 fusion.52
  160.2 1.3 collective-permute-start.8
  161.5 1.3 collective-permute-start.9
  162.8 1.0 collective-permute-done.8
  163.9 3.8 %collective-permute-done.9 = f32[8,32,15]{2,0,1:T(8,128)S(1)} collective-permute-done((f32[8,32,15]{2,0,1:T(8,128)S(1)}, f32[8,32,15]{2,0,1:T(8,128)S(1)}, u32[]{:S(2)}, u32[]{:S(2)}) %collective-permute-start.9) | collective-permute-done | bytes 15392 | tf_op jit(solution)/shard_map/ppermute | solution.py:19
  167.9 5.4 %collective-permute-start.10 = (f32[8,15,286]{2,0,1:T(8,128)S(1)}, f32[8,15,286]{2,0,1:T(8,128)S(1)}, u32[]{:S(2)}, u32[]{:S(2)}) collective-permute-start(f32[8,15,286]{2,0,1:T(8,128)S(1)} %get-tuple-element.14), channel_id=1, source_target_pairs={{0,1},{1,2},{2,3},{3,4},{4,5},{5,6},{6,7},{7,8},{8,9},{9,10},{10,1... | collective-permute-start | bytes 411848 | tf_op jit(solution)/shard_map/ppermute | solution.py:17
  173.3 1.9 collective-permute-start.11
  175.2 0.5 collective-permute-done.10
  175.8 5.3 %collective-permute-done.11 = f32[8,15,286]{2,0,1:T(8,128)S(1)} collective-permute-done((f32[8,15,286]{2,0,1:T(8,128)S(1)}, f32[8,15,286]{2,0,1:T(8,128)S(1)}, u32[]{:S(2)}, u32[]{:S(2)}) %collective-permute-start.11) | collective-permute-done | bytes 137312 | tf_op jit(solution)/shard_map/ppermute | solution.py:19
  181.1 1.4 fusion.33
  182.5 1.1 fusion.18
  183.6 0.6 fusion.46
  184.2 0.6 fusion.48
  185.1 1.3 collective-permute-start.12
  186.4 1.3 collective-permute-start.13
  187.7 2.2 collective-permute-done.12
  189.9 4.1 %collective-permute-done.13 = f32[2,8,32,15]{3,2,1,0:T(8,128)S(1)} collective-permute-done((f32[2,8,32,15]{3,2,1,0:T(8,128)S(1)}, f32[2,8,32,15]{3,2,1,0:T(8,128)S(1)}, u32[]{:S(2)}, u32[]{:S(2)}) %collective-permute-start.13) | collective-permute-done | bytes 30752 | tf_op jit(solution)/shard_map/ppermute | solution.py:19
  194.5 4.3 %collective-permute-start.14 = (f32[2,8,15,286]{3,2,1,0:T(8,128)S(1)}, f32[2,8,15,286]{3,2,1,0:T(8,128)S(1)}, u32[]{:S(2)}, u32[]{:S(2)}) collective-permute-start(f32[2,8,15,286]{3,2,1,0:T(8,128)S(1)} %get-tuple-element.6), channel_id=1, source_target_pairs={{0,1},{1,2},{2,3},{3,4},{4,5},{5,6},{6,7},{7,8},{8,9},{9,10},{10,1... | collective-permute-start | bytes 823688 | tf_op jit(solution)/shard_map/ppermute | solution.py:17
  198.7 2.1 collective-permute-start.15
  200.9 2.6 %collective-permute-done.14 = f32[2,8,15,286]{3,2,1,0:T(8,128)S(1)} collective-permute-done((f32[2,8,15,286]{3,2,1,0:T(8,128)S(1)}, f32[2,8,15,286]{3,2,1,0:T(8,128)S(1)}, u32[]{:S(2)}, u32[]{:S(2)}) %collective-permute-start.14) | collective-permute-done | bytes 274592 | tf_op jit(solution)/shard_map/ppermute | solution.py:17
  203.5 5.3 %collective-permute-done.15 = f32[2,8,15,286]{3,2,1,0:T(8,128)S(1)} collective-permute-done((f32[2,8,15,286]{3,2,1,0:T(8,128)S(1)}, f32[2,8,15,286]{3,2,1,0:T(8,128)S(1)}, u32[]{:S(2)}, u32[]{:S(2)}) %collective-permute-start.15) | collective-permute-done | bytes 274592 | tf_op jit(solution)/shard_map/ppermute | solution.py:19
  208.7 0.5 pad_maximum_fusion.1
  209.2 2.1 fusion.8
  211.3 1.1 fusion.21
  212.5 0.6 fusion.42
  213.1 0.6 fusion.44
  214.0 8.6 %all_gather.7 = f32[8,32,512]{2,0,1:T(8,128)S(1)} all-gather(f32[8,32,256]{2,0,1:T(8,128)S(1)} %fusion.61), channel_id=1, replica_groups=mesh['view'=2,'tile'=16] {'view'}, dimensions={2}, use_global_device_ids=true | all-gather | bytes 786432 | tf_op jit(solution)/shard_map/all_gather | solution.py:82
  222.6 1.1 copy.117
  (74 shorter events, 3.8 us)
Async XLA Ops:
  0.0 1.0 copy-start
  0.0 5.8 %copy-start.3 = (f32[1,8,32,512]{3,2,1,0:T(8,128)S(1)}, f32[1,8,32,512]{3,2,1,0:T(8,128)}, u32[]{:S(2)}) copy-start(f32[1,8,32,512]{3,2,1,0:T(8,128)} %param.10) | copy-start | bytes 1572868
  1.3 17.2 %collective-permute-start = (f32[8,32,15]{2,0,1:T(8,128)S(1)}, f32[8,32,15]{2,0,1:T(8,128)S(1)}, u32[]{:S(2)}, u32[]{:S(2)}) collective-permute-start(f32[8,32,15]{2,0,1:T(8,128)S(1)} %get-tuple-element.24), channel_id=1, source_target_pairs={{0,16},{1,17},{2,18},{3,19},{4,20},{5,21},{6,22},{7,23},{8,24},{9,... | collective-permute-start | bytes 46088 | tf_op jit(solution)/shard_map/ppermute | solution.py:17
  4.5 5.8 %copy-start.12 = (f32[1,3,31]{2,0,1:T(1,128)S(1)}, f32[1,3,31]{2,0,1:T(1,128)}, u32[]{:S(2)}) copy-start(f32[1,3,31]{2,0,1:T(1,128)} %param.11) | copy-start | bytes 1120
  4.5 14.0 %collective-permute-start.1 = (f32[8,32,15]{2,0,1:T(8,128)S(1)}, f32[8,32,15]{2,0,1:T(8,128)S(1)}, u32[]{:S(2)}, u32[]{:S(2)}) collective-permute-start(f32[8,32,15]{2,0,1:T(8,128)S(1)} %get-tuple-element.25), channel_id=1, source_target_pairs={{16,0},{17,1},{18,2},{19,3},{20,4},{21,5},{22,6},{23,7},{24,8},{25... | collective-permute-start | bytes 46088 | tf_op jit(solution)/shard_map/ppermute | solution.py:19
  6.7 75.5 %all-to-all-start = ((f32[2,1,8,32,256]{4,3,2,1,0:T(8,128)}), f32[2,1,8,32,256]{4,3,2,1,0:T(8,128)S(1)}, u32[]{:S(2)}, u32[]{:S(2)}) async-start(f32[2,1,8,32,256]{4,3,2,1,0:T(8,128)} %pad_maximum_fusion.4), calls=%async_computation | async-start | bytes 1048576 | tf_op jit(solution)/shard_map/all_to_all | solution.py:61
  19.4 58.0 %collective-permute-start.2 = (f32[8,15,286]{2,0,1:T(8,128)}, f32[8,15,286]{2,0,1:T(8,128)}, u32[]{:S(2)}, u32[]{:S(2)}) collective-permute-start(f32[8,15,286]{2,0,1:T(8,128)} %get-tuple-element.20), channel_id=1, source_target_pairs={{0,1},{1,2},{2,3},{3,4},{4,5},{5,6},{6,7},{7,8},{8,9},{9,10},{10,1... | collective-permute-start | bytes 411848 | tf_op jit(solution)/shard_map/ppermute | solution.py:17
  24.3 53.1 %collective-permute-start.3 = (f32[8,15,286]{2,0,1:T(8,128)S(1)}, f32[8,15,286]{2,0,1:T(8,128)}, u32[]{:S(2)}, u32[]{:S(2)}) collective-permute-start(f32[8,15,286]{2,0,1:T(8,128)S(1)} %get-tuple-element.21), channel_id=1, source_target_pairs={{1,0},{2,1},{3,2},{4,3},{5,4},{6,5},{7,6},{8,7},{9,8},{10,9},{11,1... | collective-permute-start | bytes 411848 | tf_op jit(solution)/shard_map/ppermute | solution.py:19
  26.3 51.2 %copy-start.8 = (pred[8,8]{1,0:T(8,128)(4,1)}, pred[8,8]{1,0:T(8,128)(4,1)S(1)}, u32[]{:S(2)}) copy-start(pred[8,8]{1,0:T(8,128)(4,1)S(1)} %get-tuple-element.29) | copy-start | bytes 196
  26.3 51.2 %copy-start.10 = (pred[8,8]{1,0:T(8,128)(4,1)}, pred[8,8]{1,0:T(8,128)(4,1)S(1)}, u32[]{:S(2)}) copy-start(pred[8,8]{1,0:T(8,128)(4,1)S(1)} %get-tuple-element.30) | copy-start | bytes 196
  27.2 50.2 %copy-start.5 = (f32[8,8,2]{1,0,2:T(8,128)}, f32[8,8,2]{1,0,2:T(8,128)S(1)}, u32[]{:S(2)}) copy-start(f32[8,8,2]{1,0,2:T(8,128)S(1)} %copy.129) | copy-start | bytes 1540
  82.5 6.5 %collective-permute-start.4 = (f32[2,8,32,15]{3,2,1,0:T(8,128)S(1)}, f32[2,8,32,15]{3,2,1,0:T(8,128)S(1)}, u32[]{:S(2)}, u32[]{:S(2)}) collective-permute-start(f32[2,8,32,15]{3,2,1,0:T(8,128)S(1)} %get-tuple-element.16), channel_id=1, source_target_pairs={{0,16},{1,17},{2,18},{3,19},{4,20},{5,21},{6,22},{7,23},{8,24},{9,... | collective-permute-start | bytes 92168 | tf_op jit(solution)/shard_map/ppermute | solution.py:17
  83.9 8.9 %collective-permute-start.5 = (f32[2,8,32,15]{3,2,1,0:T(8,128)S(1)}, f32[2,8,32,15]{3,2,1,0:T(8,128)S(1)}, u32[]{:S(2)}, u32[]{:S(2)}) collective-permute-start(f32[2,8,32,15]{3,2,1,0:T(8,128)S(1)} %get-tuple-element.17), channel_id=1, source_target_pairs={{16,0},{17,1},{18,2},{19,3},{20,4},{21,5},{22,6},{23,7},{24,8},{25... | collective-permute-start | bytes 92168 | tf_op jit(solution)/shard_map/ppermute | solution.py:19
  92.8 1.3 copy-start.1
  94.2 59.4 %collective-permute-start.6 = (f32[2,8,15,286]{3,2,1,0:T(8,128)}, f32[2,8,15,286]{3,2,1,0:T(8,128)}, u32[]{:S(2)}, u32[]{:S(2)}) collective-permute-start(f32[2,8,15,286]{3,2,1,0:T(8,128)} %get-tuple-element.10), channel_id=1, source_target_pairs={{0,1},{1,2},{2,3},{3,4},{4,5},{5,6},{6,7},{7,8},{8,9},{9,10},{10,1... | collective-permute-start | bytes 823688 | tf_op jit(solution)/shard_map/ppermute | solution.py:17
  98.9 54.7 %collective-permute-start.7 = (f32[2,8,15,286]{3,2,1,0:T(8,128)}, f32[2,8,15,286]{3,2,1,0:T(8,128)}, u32[]{:S(2)}, u32[]{:S(2)}) collective-permute-start(f32[2,8,15,286]{3,2,1,0:T(8,128)} %get-tuple-element.11), channel_id=1, source_target_pairs={{1,0},{2,1},{3,2},{4,3},{5,4},{6,5},{7,6},{8,7},{9,8},{10,9},{11,1... | collective-permute-start | bytes 823688 | tf_op jit(solution)/shard_map/ppermute | solution.py:19
  147.5 6.0 %copy-start.2 = (f32[2,8,32,15]{3,2,1,0:T(8,128)S(1)}, f32[2,8,32,15]{3,2,1,0:T(8,128)}, u32[]{:S(2)}) copy-start(f32[2,8,32,15]{3,2,1,0:T(8,128)} %copy-done.1) | copy-start | bytes 92164
  153.5 1.6 copy-start.7
  153.6 1.6 copy-start.9
  153.6 1.6 copy-start.11
  155.2 2.1 copy-start.4
  159.7 21.4 %copy-start.6 = (f32[8,8,2]{1,0,2:T(8,128)S(1)}, f32[8,8,2]{1,0,2:T(8,128)}, u32[]{:S(2)}) copy-start(f32[8,8,2]{1,0,2:T(8,128)} %copy-done.5) | copy-start | bytes 1540
  160.2 3.6 %collective-permute-start.8 = (f32[8,32,15]{2,0,1:T(8,128)S(1)}, f32[8,32,15]{2,0,1:T(8,128)S(1)}, u32[]{:S(2)}, u32[]{:S(2)}) collective-permute-start(f32[8,32,15]{2,0,1:T(8,128)S(1)} %get-tuple-element.22), channel_id=1, source_target_pairs={{0,16},{1,17},{2,18},{3,19},{4,20},{5,21},{6,22},{7,23},{8,24},{9,... | collective-permute-start | bytes 46088 | tf_op jit(solution)/shard_map/ppermute | solution.py:17
  161.5 6.1 %collective-permute-start.9 = (f32[8,32,15]{2,0,1:T(8,128)S(1)}, f32[8,32,15]{2,0,1:T(8,128)S(1)}, u32[]{:S(2)}, u32[]{:S(2)}) collective-permute-start(f32[8,32,15]{2,0,1:T(8,128)S(1)} %get-tuple-element.23), channel_id=1, source_target_pairs={{16,0},{17,1},{18,2},{19,3},{20,4},{21,5},{22,6},{23,7},{24,8},{25... | collective-permute-start | bytes 46088 | tf_op jit(solution)/shard_map/ppermute | solution.py:19
  167.9 7.9 %collective-permute-start.10 = (f32[8,15,286]{2,0,1:T(8,128)S(1)}, f32[8,15,286]{2,0,1:T(8,128)S(1)}, u32[]{:S(2)}, u32[]{:S(2)}) collective-permute-start(f32[8,15,286]{2,0,1:T(8,128)S(1)} %get-tuple-element.14), channel_id=1, source_target_pairs={{0,1},{1,2},{2,3},{3,4},{4,5},{5,6},{6,7},{7,8},{8,9},{9,10},{10,1... | collective-permute-start | bytes 411848 | tf_op jit(solution)/shard_map/ppermute | solution.py:17
  173.3 7.8 %collective-permute-start.11 = (f32[8,15,286]{2,0,1:T(8,128)S(1)}, f32[8,15,286]{2,0,1:T(8,128)S(1)}, u32[]{:S(2)}, u32[]{:S(2)}) collective-permute-start(f32[8,15,286]{2,0,1:T(8,128)S(1)} %get-tuple-element.15), channel_id=1, source_target_pairs={{1,0},{2,1},{3,2},{4,3},{5,4},{6,5},{7,6},{8,7},{9,8},{10,9},{11,1... | collective-permute-start | bytes 411848 | tf_op jit(solution)/shard_map/ppermute | solution.py:19
  185.1 4.8 %collective-permute-start.12 = (f32[2,8,32,15]{3,2,1,0:T(8,128)S(1)}, f32[2,8,32,15]{3,2,1,0:T(8,128)S(1)}, u32[]{:S(2)}, u32[]{:S(2)}) collective-permute-start(f32[2,8,32,15]{3,2,1,0:T(8,128)S(1)} %get-tuple-element.12), channel_id=1, source_target_pairs={{0,16},{1,17},{2,18},{3,19},{4,20},{5,21},{6,22},{7,23},{8,24},{9,... | collective-permute-start | bytes 92168 | tf_op jit(solution)/shard_map/ppermute | solution.py:17
  186.4 7.6 %collective-permute-start.13 = (f32[2,8,32,15]{3,2,1,0:T(8,128)S(1)}, f32[2,8,32,15]{3,2,1,0:T(8,128)S(1)}, u32[]{:S(2)}, u32[]{:S(2)}) collective-permute-start(f32[2,8,32,15]{3,2,1,0:T(8,128)S(1)} %get-tuple-element.13), channel_id=1, source_target_pairs={{16,0},{17,1},{18,2},{19,3},{20,4},{21,5},{22,6},{23,7},{24,8},{25... | collective-permute-start | bytes 92168 | tf_op jit(solution)/shard_map/ppermute | solution.py:19
  194.5 9.0 %collective-permute-start.14 = (f32[2,8,15,286]{3,2,1,0:T(8,128)S(1)}, f32[2,8,15,286]{3,2,1,0:T(8,128)S(1)}, u32[]{:S(2)}, u32[]{:S(2)}) collective-permute-start(f32[2,8,15,286]{3,2,1,0:T(8,128)S(1)} %get-tuple-element.6), channel_id=1, source_target_pairs={{0,1},{1,2},{2,3},{3,4},{4,5},{5,6},{6,7},{7,8},{8,9},{9,10},{10,1... | collective-permute-start | bytes 823688 | tf_op jit(solution)/shard_map/ppermute | solution.py:17
  198.7 10.0 %collective-permute-start.15 = (f32[2,8,15,286]{3,2,1,0:T(8,128)S(1)}, f32[2,8,15,286]{3,2,1,0:T(8,128)S(1)}, u32[]{:S(2)}, u32[]{:S(2)}) collective-permute-start(f32[2,8,15,286]{3,2,1,0:T(8,128)S(1)} %get-tuple-element.8), channel_id=1, source_target_pairs={{1,0},{2,1},{3,2},{4,3},{5,4},{6,5},{7,6},{8,7},{9,8},{10,9},{11,1... | collective-permute-start | bytes 823688 | tf_op jit(solution)/shard_map/ppermute | solution.py:19
